TPU v7x, 512 devices: a whole 4x4x16 slice. The times are simulated.
512 devices in a mesh: guide: 2 (over x_lo), seq: 32 (over x_hi, z), blk: 8 (over y, core).
Axes of the slice: x: 4 (x_hi: 2, x_lo: 2; x = x_hi * 2 + x_lo), y: 4, z: 16, core: 2. Of those that a mesh axis runs over, the one named last changes fastest.
Arguments:
- img_hidden: bfloat16 [2, 2, 2048, 3072], P('guide', None, 'seq', 'blk'), may hold values from -6 to 6
- img_query: bfloat16 [2, 2, 2048, 3072], P('guide', None, 'seq', 'blk')
- img_key: bfloat16 [2, 2, 2048, 3072], P('guide', None, 'seq', 'blk')
- img_value: bfloat16 [2, 2, 2048, 3072], P('guide', None, 'seq', 'blk'), may hold values from -6 to 6
- txt_key: bfloat16 [2, 2, 512, 3072], P('guide', None, 'seq', 'blk'), may hold values from -6 to 6
- txt_value: bfloat16 [2, 2, 512, 3072], P('guide', None, 'seq', 'blk'), may hold values from -6 to 6
- query_gain: float32 [128], replicated
- key_gain: float32 [2, 128], replicated
- gate: float32 [2, 2, 3072], P('guide', None, 'blk'), may hold values from -4 to 4
- proj_weight: bfloat16 [3072, 3072], P('blk'), may hold values from -0.15625 to 0.15625
- proj_bias: float32 [3072], P('blk'), may hold values from -3 to 3
- guidance: float32 [2], replicated, may hold values from 1.5 to 5
- text_len: int32 [2], replicated, may hold values from 1 to 512, as said below
- step_index: int32 [1], replicated, may hold values from 0 to 7
- latent: bfloat16 [2, 2048, 3072], P('guide', 'seq', 'blk'), may hold values from -6 to 6
Outputs:
- guided: bfloat16 [2, 2048, 3072], P('guide', 'seq', 'blk')
- next_state: bfloat16 [2, 2048, 3072], P('guide', 'seq', 'blk')
Inputs may be any that keep to these rules, and one draw needn't show every extreme that they name: `text_len`: some prompt has all 512 text slots live.
All inputs are finite; a program needn't handle non-finite values.
Results may differ from a plain program's by a relative error of at most 0.0095.
Values may be sent and summed in bfloat16 or wider, within the bound.
No kernel may reach another device: no remote copies, remote signals or barrier semaphores. Data moves between devices by JAX's collectives and lax.ppermute only.
A program may use at most 64 MiB of HBM per device.

v0:
```python
import jax
import jax.numpy as jnp
from jax import lax
from jax.sharding import PartitionSpec as P

HD = 128
GRID = 64
STEPS = 8


def rope_angles(positions):
    first = HD // 8
    second = (HD - first) // 2
    freqs = 10000.0 ** (-jnp.arange(0, second, 2).astype(jnp.float32) / second)
    rows = (positions // GRID).astype(jnp.float32)
    cols = (positions % GRID).astype(jnp.float32)
    zeros = jnp.zeros((positions.shape[0], first // 2), jnp.float32)
    return jnp.concatenate([zeros, rows[:, None] * freqs, cols[:, None] * freqs], -1)


def rotate(values, angles):
    pairs = values.reshape(values.shape[:-1] + (HD // 2, 2))
    cosine = jnp.cos(angles)[None, :, None, :]
    sine = jnp.sin(angles)[None, :, None, :]
    first = pairs[..., 0] * cosine - pairs[..., 1] * sine
    second = pairs[..., 0] * sine + pairs[..., 1] * cosine
    return jnp.stack([first, second], -1).reshape(values.shape)


def normed(values, gain_row):
    heads = values.astype(jnp.float32).reshape(
        values.shape[0], values.shape[1], values.shape[2] // HD, HD
    )
    return heads / jnp.sqrt(jnp.mean(heads * heads, -1, keepdims=True) + 1e-06) * gain_row


def shards(
    img_hidden,
    img_query,
    img_key,
    img_value,
    txt_key,
    txt_value,
    query_gain,
    key_gain,
    gate,
    proj_weight,
    proj_bias,
    guidance,
    text_len,
    step_index,
    latent,
):
    prompts = img_query.shape[1]
    img_here = img_query.shape[2]
    txt_here = txt_key.shape[2]
    width_here = img_query.shape[3]
    heads_here = width_here // HD
    slot_here = img_here + txt_here
    positions = lax.axis_index("seq") * img_here + jnp.arange(img_here)
    angles = rope_angles(positions)
    queries = rotate(normed(img_query[0], query_gain), angles).astype(jnp.bfloat16)
    keys_img = rotate(normed(img_key[0], key_gain[0]), angles).astype(jnp.bfloat16)
    keys_txt = normed(txt_key[0], key_gain[1]).astype(jnp.bfloat16)
    keys_local = jnp.concatenate([keys_txt, keys_img], 1).reshape(prompts, slot_here, width_here)
    values_local = jnp.concatenate([txt_value[0], img_value[0]], 1)
    running = jnp.full((prompts, img_here, heads_here), -1e30, jnp.float32)
    key_piece = lax.all_gather(keys_local, "seq", axis=1, tiled=True)
    value_piece = lax.all_gather(values_local, "seq", axis=1, tiled=True)
    count = key_piece.shape[1]
    index = jnp.arange(count)
    device = index // slot_here
    within = index % slot_here
    text_pos = device * txt_here + within
    live = (within >= txt_here)[None, :] | (text_pos[None, :] < text_len[:, None])
    key_heads = key_piece.reshape(prompts, count, heads_here, HD)
    value_heads = value_piece.reshape(prompts, count, heads_here, HD)
    scores = jnp.einsum(
        "pqhd,pkhd->pqhk", queries, key_heads, preferred_element_type=jnp.float32
    ) * HD ** (-0.5)
    mask = live[:, None, None, :]
    scores = jnp.where(mask, scores, -1e30)
    newest = jnp.maximum(running, jnp.max(scores, -1))
    expo = jnp.where(mask, jnp.exp(scores - newest[..., None]), 0.0)
    total = jnp.sum(expo, -1)
    accum = jnp.einsum(
        "pqhk,pkhd->pqhd",
        expo.astype(jnp.bfloat16),
        value_heads,
        preferred_element_type=jnp.float32,
    )
    running, total, accum = (newest, total, accum)
    attn = (accum / total[..., None]).astype(jnp.bfloat16).reshape(prompts * img_here, width_here)
    partial_value = jnp.dot(attn, proj_weight, preferred_element_type=jnp.float32)
    proj = lax.psum_scatter(
        partial_value.astype(jnp.bfloat16), "blk", scatter_dimension=1, tiled=True
    ).astype(jnp.float32)
    proj = (proj + proj_bias).reshape(prompts, img_here, width_here)
    layer_out = (img_hidden[0].astype(jnp.float32) + gate[0][:, None, :] * proj).astype(
        jnp.bfloat16
    )
    both_halves = lax.all_to_all(layer_out[None], "guide", split_axis=1, concat_axis=0, tiled=True)
    cond = both_halves[0].astype(jnp.float32)
    uncond = both_halves[1].astype(jnp.float32)
    own_prompts = cond.shape[0]
    scale_here = lax.dynamic_slice_in_dim(
        guidance, lax.axis_index("guide") * own_prompts, own_prompts, 0
    )
    guided_f = uncond + scale_here[:, None, None] * (cond - uncond)
    index = step_index[0]
    u_now = 1.0 - index.astype(jnp.float32) / STEPS
    u_next = 1.0 - (index + 1).astype(jnp.float32) / STEPS
    step_size = 3.0 * u_next / (1.0 + 2.0 * u_next) - 3.0 * u_now / (1.0 + 2.0 * u_now)
    next_state = (latent.astype(jnp.float32) + step_size * guided_f).astype(jnp.bfloat16)
    return (guided_f.astype(jnp.bfloat16), next_state)


def solution(mesh):
    return jax.shard_map(
        shards,
        mesh=mesh,
        in_specs=(
            P("guide", None, "seq", "blk"),
            P("guide", None, "seq", "blk"),
            P("guide", None, "seq", "blk"),
            P("guide", None, "seq", "blk"),
            P("guide", None, "seq", "blk"),
            P("guide", None, "seq", "blk"),
            P(),
            P(),
            P("guide", None, "blk"),
            P("blk", None),
            P("blk"),
            P(),
            P(),
            P(),
            P("guide", "seq", "blk"),
        ),
        out_specs=(P("guide", "seq", "blk"), P("guide", "seq", "blk")),
        check_vma=False,
    )
```

profile of v0, /device:TPU:4, one launch (start us, length us, event | category | flops | bytes accessed | tf_op | source)
XLA Modules:
  0.0 420.7 jit_solution(10959240967538015908)
XLA Ops:
  7.2 0.0 copy-start
  7.2 0.0 copy-start.4
  7.2 0.0 all-gather.5.cloned.1.call-start
  7.2 0.6 multiply_power_fusion
  7.8 1.6 convert_multiply_fusion.1
  9.5 1.0 copy.58
  10.5 1.6 convert_multiply_fusion.2
  12.1 1.0 copy.52
  13.1 0.6 fusion.35
  13.7 0.8 slice_bitcast_fusion.2
  14.5 0.1 mul.268
  14.6 1.0 mul.267
  15.6 0.2 reduce_sum.37
  15.9 0.7 copy.54
  16.6 1.0 mul.285
  17.6 0.2 reduce_sum.38
  17.8 0.0 copy-start.2
  17.8 0.7 copy.60
  18.5 0.8 mul.286
  19.3 0.7 convert_multiply_fusion
  20.1 0.1 reduce_sum.36
  20.2 0.1 div.91
  20.3 0.0 copy-done.4
  20.4 0.2 copy.55
  20.6 0.8 broadcast_multiply_fusion.1
  21.3 0.2 fusion.26
  21.5 1.1 divide_multiply_fusion
  22.7 1.0 subtract_convert_fusion
  23.7 0.5 pad_maximum_fusion
  24.2 0.1 pad_maximum_fusion.1
  24.4 0.8 copy.56
  25.2 0.0 all-gather.5.cloned.1.call-update
  25.2 0.0 all-gather.3.cloned.1.call-start
  25.2 0.1 copy.82
  25.4 0.8 copy.83
  26.1 0.8 pad_maximum_fusion.3
  26.9 0.0 all-gather.3.cloned.1.call-update
  27.0 0.0 reduce-scatter.4.cloned.1.call-start
  27.0 0.5 pad_maximum_fusion.2
  27.6 0.7 compare_or_fusion
  28.3 161.3 %all-gather.5.cloned.1.call-done = bf16[2,2560,384]{2,0,1:T(2,128)(2,1)} async-done(((bf16[2,80,384]{2,0,1:T(2,128)(2,1)}), bf16[2,2560,384]{2,0,1:T(2,128)(2,1)}) %all-gather.5.cloned.1.call-update) | async-done | bytes 3932176 | tf_op jit(solution)/shard_map/all_gather | solution.py:68
  189.6 10.5 %copy.57 = bf16[2,2560,384]{1,2,0:T(8,128)(2,1)} copy(bf16[2,2560,384]{2,0,1:T(2,128)(2,1)} %all-gather.5.cloned.1.call-done) | data formatting | bytes 7864320 | tf_op jit(solution)/shard_map/all_gather | solution.py:68
  200.1 3.2 fusion.38
  203.4 1.9 copy-done.1
  205.2 0.9 fusion.2
  206.1 143.7 %all-gather.3.cloned.1.call-done = bf16[2,2560,384]{2,0,1:T(2,128)(2,1)} async-done(((bf16[2,80,384]{2,0,1:T(2,128)(2,1)}), bf16[2,2560,384]{2,0,1:T(2,128)(2,1)}) %all-gather.3.cloned.1.call-update) | async-done | bytes 3932176 | tf_op jit(solution)/shard_map/all_gather | solution.py:69
  349.8 10.5 %copy.51 = bf16[2,2560,384]{1,2,0:T(8,128)(2,1)} copy(bf16[2,2560,384]{2,0,1:T(2,128)(2,1)} %all-gather.3.cloned.1.call-done) | data formatting | bytes 7864320 | tf_op jit(solution)/shard_map/all_gather | solution.py:69
  360.3 4.8 %fusion.15 = bf16[2,64,3,128]{3,1,2,0:T(8,128)(2,1)S(1)} fusion(bf16[2,2560,3,128]{1,3,2,0:T(8,128)(2,1)} %bitcast.73, f32[2,64,3,2560]{3,1,2,0:T(8,128)} %copy-done.1, f32[2,64,3]{1,2,0:T(4,128)S(1)} %broadcast_maximum_fusion, pred[2,2560]{1,0:T(4,128)(4,1)S(1)} %compare_or_fusion, f32[2,64,3]{1,2,0:T(4,128)S(1)} %fusion.2), kind=kOutput, calls=%fused_computation.13 | convolution fusion | flops 254705664 | bytes 7970816 | tf_op jit(solution)/shard_map/pqhk,pkhd->pqhd/dot_general | solution.py:86
  365.1 0.0 copy-start.7
  365.1 0.0 copy-start.3
  365.2 0.0 copy-start.6
  365.2 0.0 copy-start.8
  365.2 0.0 copy-start.5
  365.2 0.1 copy.64
  365.3 0.6 convolution_convert_fusion
  365.9 1.2 copy.69
  367.0 0.0 reduce-scatter.4.cloned.1.call-update
  367.1 36.4 %reduce-scatter.4.cloned.1.call-done = bf16[384,128]{1,0:T(8,128)(2,1)} async-done(((bf16[3072,128]{1,0:T(8,128)(2,1)}), bf16[384,128]{1,0:T(8,128)(2,1)}) %reduce-scatter.4.cloned.1.call-update) | async-done | bytes 98320
  403.5 1.0 copy.70
  404.5 0.7 add_convert_fusion
  405.2 3.3 all-to-all-start
  409.2 0.6 dynamic_slice.3
  409.9 2.9 all-to-all-done
  412.8 1.3 add_convert_fusion.3
  (21 shorter events, 0.2 us)
Async XLA Ops:
  7.2 358.1 %copy-start = (bf16[384,3072]{1,0:T(8,128)(2,1)S(1)}, bf16[384,3072]{1,0:T(8,128)(2,1)}, u32[]{:S(2)}) copy-start(bf16[384,3072]{1,0:T(8,128)(2,1)} %param.24) | copy-start | bytes 7077892
  7.2 13.2 %copy-start.4 = (bf16[1,2,16,384]{3,2,1,0:T(8,128)(2,1)S(1)}, bf16[1,2,16,384]{3,2,1,0:T(8,128)(2,1)}, u32[]{:S(2)}) copy-start(bf16[1,2,16,384]{3,2,1,0:T(8,128)(2,1)} %param.19) | copy-start | bytes 73732
  7.2 182.4 %all-gather.5.cloned.1.call-start = ((), (), s32[]{:S(2)}) async-start(), calls=%async_computation.3 | async-start | bytes 4055040 | tf_op jit(solution)/shard_map/all_gather | solution.py:68
  17.8 7.4 %copy-start.2 = (bf16[1,2,64,384]{3,2,1,0:T(8,128)(2,1)S(1)}, bf16[1,2,64,384]{3,2,1,0:T(8,128)(2,1)}, u32[]{:S(2)}) copy-start(bf16[1,2,64,384]{3,2,1,0:T(8,128)(2,1)} %param.18) | copy-start | bytes 294916
  25.2 324.6 %all-gather.3.cloned.1.call-start = ((), (), s32[]{:S(2)}) async-start(), calls=%async_computation.2 | async-start | bytes 4055040 | tf_op jit(solution)/shard_map/all_gather | solution.py:69
  27.0 376.5 %reduce-scatter.4.cloned.1.call-start = ((), (), s32[]{:S(2)}) async-start(), calls=%async_computation.4 | async-start | bytes 884736
  203.3 1.9 copy-start.1
  365.1 39.4 %copy-start.7 = (f32[384]{0:T(512)S(1)}, f32[384]{0:T(512)}, u32[]{:S(2)}) copy-start(f32[384]{0:T(512)} %param.25) | copy-start | bytes 4612
  365.1 39.4 %copy-start.3 = (bf16[1,2,64,384]{3,2,1,0:T(8,128)(2,1)S(1)}, bf16[1,2,64,384]{3,2,1,0:T(8,128)(2,1)}, u32[]{:S(2)}) copy-start(bf16[1,2,64,384]{3,2,1,0:T(8,128)(2,1)} %param.15) | copy-start | bytes 294916
  365.2 39.4 %copy-start.6 = (f32[1,2,384]{2,1,0:T(2,128)S(1)}, f32[1,2,384]{2,1,0:T(2,128)}, u32[]{:S(2)}) copy-start(f32[1,2,384]{2,1,0:T(2,128)} %param.23) | copy-start | bytes 9220
  365.2 44.1 %copy-start.8 = (f32[2]{0:T(128)S(1)}, f32[2]{0:T(128)}, u32[]{:S(2)}) copy-start(f32[2]{0:T(128)} %param.26) | copy-start | bytes 28
  365.2 47.7 %copy-start.5 = (bf16[1,64,384]{2,1,0:T(8,128)(2,1)S(1)}, bf16[1,64,384]{2,1,0:T(8,128)(2,1)}, u32[]{:S(2)}) copy-start(bf16[1,64,384]{2,1,0:T(8,128)(2,1)} %param.29) | copy-start | bytes 147460
  405.2 7.6 %all-to-all-start = ((bf16[1,2,64,384]{3,2,0,1:T(8,128)(2,1)}), bf16[1,2,64,384]{3,2,0,1:T(8,128)(2,1)S(1)}, u32[]{:S(2)}, u32[]{:S(2)}) async-start(bf16[1,2,64,384]{3,2,0,1:T(8,128)(2,1)} %add_convert_fusion), calls=%async_computation | async-start | bytes 196608 | tf_op jit(solution)/shard_map/all_to_all | solution.py:102
Sparse Core Ops, SparseCore 0:
  25.3 164.2 all-gather.4
  192.7 157.0 all-gather.2
  367.2 36.2 reduce-scatter.3
where the time goes:
time: 422 us; the launch traced here: 421 us
  waiting for transfers between devices  344 us (82%)
  local copies, waits for them, and re-layouts  35 us (8%)
  between operations  14.9 us (4%)
  other arithmetic  14.5 us (3%)
  matrix products  8.61 us (2%)
    all_gather x1, waiting for transfers between devices, shards(): key_piece = lax.all_gather(keys_local, 'seq', axis=1, tiled=True)  161 us
    all_gather x1, waiting for transfers between devices, shards(): value_piece = lax.all_gather(values_local, 'seq', axis=1, tiled=True)  144 us
    unnamed x4, waiting for transfers between devices  36.5 us
    all_gather x1, local copies, waits for them, and re-layouts, shards(): value_piece = lax.all_gather(values_local, 'seq', axis=1, tiled=True)  10.5 us
    all_gather x1, local copies, waits for them, and re-layouts, shards(): key_piece = lax.all_gather(keys_local, 'seq', axis=1, tiled=True)  10.5 us
  transfers between devices with their start and end apart: 4, of which 4 were waited for; matrix products, arithmetic and copies ran while one was open for 4% of the time, Pallas kernels for 0%

commit v1 on v0

--- a/solution.py
+++ b/solution.py
@@ -66,7 +66,12 @@
     values_local = jnp.concatenate([txt_value[0], img_value[0]], 1)
     running = jnp.full((prompts, img_here, heads_here), -1e30, jnp.float32)
     key_piece = lax.all_gather(keys_local, "seq", axis=1, tiled=True)
-    value_piece = lax.all_gather(values_local, "seq", axis=1, tiled=True)
+    value_piece = jnp.concatenate(
+        lax.all_to_all(
+            jnp.stack([values_local for _ in range(lax.axis_size("seq"))], axis=0), "seq", 0, 0
+        ),
+        axis=1,
+    )
     count = key_piece.shape[1]
     index = jnp.arange(count)
     device = index // slot_here

time: 422 us -> 347 us (0.82)
  waiting for transfers between devices: 344 us -> 257 us
  starting transfers between devices: 3.46 us -> 21.8 us
  other arithmetic: 14.5 us -> 8.19 us
    all_gather x1 -> x0, waiting for transfers between devices: 144 us -> none  [shards(): value_piece = lax.all_gather(values_local, 'seq', axis=1, tiled=True)]
    all_gather x1, waiting for transfers between devices: 161 us -> 218 us  [shards(): key_piece = lax.all_gather(keys_local, 'seq', axis=1, tiled=True)]
    all_to_all x0 -> x1, starting transfers between devices: none -> 18.4 us  [shards(): lax.all_to_all(jnp.stack([values_local for _ in range(lax.axis_size('seq'...]
    another operation x0 -> x2, local copies, waits for them, and re-layouts: none -> 13.1 us  [the longest x1 10.9 us: shards(): value_heads = value_piece.reshape(prompts, count, heads_here, HD)]
    all_gather x1 -> x0, local copies, waits for them, and re-layouts: 10.5 us -> none  [shards(): value_piece = lax.all_gather(values_local, 'seq', axis=1, tiled=True)]
    reshape x0 -> x1, local copies, waits for them, and re-layouts: none -> 4.45 us  [shards(): jnp.concatenate(lax.all_to_all(jnp.stack([values_local for _ in range(lax...]
    unnamed x4 -> x3, waiting for transfers between devices: 36.5 us -> 36.2 us
  transfers between devices with their start and end apart: 4 -> 4, of which waited for: 4 -> 3; matrix products, arithmetic and copies ran while one was open for 4% -> 6% of each run, Pallas kernels for 0% -> 0%
where the time goes in v1:
time: 347 us; the launch traced here: 346 us
  waiting for transfers between devices  257 us (74%)
  local copies, waits for them, and re-layouts  35.9 us (10%)
  starting transfers between devices  21.8 us (6%)
  between operations  15.2 us (4%)
  matrix products  8.61 us (2%)
  other arithmetic  8.19 us (2%)
    all_gather x1, waiting for transfers between devices, shards(): key_piece = lax.all_gather(keys_local, 'seq', axis=1, tiled=True)  218 us
    unnamed x3, waiting for transfers between devices  36.2 us
    all_to_all x1, starting transfers between devices, shards(): lax.all_to_all(jnp.stack([values_local for _ in range(lax.axis_size('seq'...  18.4 us
    another operation x1, local copies, waits for them, and re-layouts, shards(): value_heads = value_piece.reshape(prompts, count, heads_here, HD)  10.9 us
    all_gather x1, local copies, waits for them, and re-layouts, shards(): key_piece = lax.all_gather(keys_local, 'seq', axis=1, tiled=True)  10.6 us
  transfers between devices with their start and end apart: 4, of which 3 were waited for; matrix products, arithmetic and copies ran while one was open for 6% of the time, Pallas kernels for 0%

profile of v1, /device:TPU:4, one launch (start us, length us, event | category | flops | bytes accessed | tf_op | source)
XLA Modules:
  0.0 346.4 jit_solution(17675082361574705458)
XLA Ops:
  7.2 0.0 copy-start
  7.2 1.1 pad_maximum_fusion.3
  8.2 2.2 stack.8
  10.5 0.0 copy-start.5
  10.5 18.4 %all-to-all-start = ((bf16[32,2,80,384]{3,2,1,0:T(8,128)(2,1)}), bf16[32,2,80,384]{3,2,1,0:T(8,128)(2,1)}, u32[]{:S(2)}, u32[]{:S(2)}) async-start(bf16[32,2,80,384]{3,2,1,0:T(8,128)(2,1)} %stack.8), calls=%async_computation | async-start | bytes 7864320 | tf_op jit(solution)/shard_map/all_to_all | solution.py:70
  28.9 0.0 all-gather.2.cloned.1.call-start
  29.0 0.0 copy-done.9
  29.0 0.1 mul.268
  29.1 0.0 copy-done.2
  29.1 0.1 copy.46
  29.3 0.1 mul.267
  29.4 0.2 reduce_sum.37
  29.7 0.1 copy.48
  29.7 0.0 copy-done.3
  29.7 0.1 copy.52
  29.9 0.0 copy-start.11
  29.9 0.7 convert_multiply_fusion.1
  30.6 1.0 mul.285
  31.6 0.2 reduce_sum.38
  31.9 0.1 copy.54
  31.9 0.0 copy-done.10
  31.9 0.1 mul.286
  32.1 0.0 copy-done.5
  32.1 0.1 reduce_sum.36
  32.3 0.1 div.91
  32.4 0.2 copy.49
  32.7 0.1 broadcast_multiply_fusion.1
  32.7 0.2 fusion.33
  32.9 0.4 divide_multiply_fusion
  33.4 1.0 subtract_convert_fusion
  34.4 0.5 pad_maximum_fusion
  34.9 0.1 pad_maximum_fusion.1
  35.1 0.8 copy.50
  35.9 0.0 all-gather.2.cloned.1.call-update
  35.9 0.0 reduce-scatter.4.cloned.1.call-start
  36.0 0.5 pad_maximum_fusion.2
  36.5 0.0 copy-done.11
  36.5 0.1 compare_or_fusion
  36.6 217.5 %all-gather.2.cloned.1.call-done = bf16[2,2560,384]{2,0,1:T(2,128)(2,1)} async-done(((bf16[2,80,384]{2,0,1:T(2,128)(2,1)}), bf16[2,2560,384]{2,0,1:T(2,128)(2,1)}) %all-gather.2.cloned.1.call-update) | async-done | bytes 3932176 | tf_op jit(solution)/shard_map/all_gather | solution.py:68
  254.2 10.6 %copy.51 = bf16[2,2560,384]{1,2,0:T(8,128)(2,1)} copy(bf16[2,2560,384]{2,0,1:T(2,128)(2,1)} %all-gather.2.cloned.1.call-done) | data formatting | bytes 7864320 | tf_op jit(solution)/shard_map/all_gather | solution.py:68
  264.7 3.2 fusion.45
  268.0 2.0 copy-done.1
  269.9 0.9 fusion.4
  270.8 0.0 all-to-all-done
  270.8 4.5 %copy.45 = bf16[2,32,80,384]{3,2,1,0:T(8,128)(2,1)} copy(bf16[2,32,80,384]{3,2,0,1:T(8,128)(2,1)} %bitcast.4) | data formatting | bytes 7864320 | tf_op jit(solution)/shard_map/reshape | solution.py:69
  275.2 10.9 %reshape_reshape.3 = bf16[2,2560,3,128]{3,2,1,0:T(4,128)(2,1)} reshape(bf16[2,32,80,384]{3,2,1,0:T(8,128)(2,1)} %copy.45) | data formatting | bytes 7864320 | tf_op jit(solution)/shard_map/reshape;reshape | solution.py:82
  286.1 4.8 %fusion.20 = bf16[2,64,3,128]{3,1,2,0:T(8,128)(2,1)S(1)} fusion(bf16[2,2560,3,128]{3,2,1,0:T(4,128)(2,1)} %reshape_reshape.3, f32[2,64,3,2560]{3,1,2,0:T(8,128)} %copy-done.1, f32[2,64,3]{1,2,0:T(4,128)S(1)} %broadcast_maximum_fusion, pred[2,2560]{1,0:T(4,128)(4,1)S(1)} %compare_or_fusion, f32[2,64,3]{1,2,0:T(4,128)S(1)} %fusion.4), kind=kOutput, calls=%fused_computation.14 | convolution fusion | flops 254705664 | bytes 7970816 | tf_op jit(solution)/shard_map/pqhk,pkhd->pqhd/dot_general | solution.py:91
  290.9 0.0 copy-start.8
  290.9 0.0 copy-start.4
  290.9 0.0 copy-start.7
  291.0 0.0 copy-start.12
  291.0 0.0 copy-start.6
  291.0 0.1 copy.58
  291.1 0.0 copy-done
  291.1 0.6 convolution_convert_fusion
  291.7 1.2 copy.62
  292.8 0.0 reduce-scatter.4.cloned.1.call-update
  292.8 36.2 %reduce-scatter.4.cloned.1.call-done = bf16[384,128]{1,0:T(8,128)(2,1)} async-done(((bf16[3072,128]{1,0:T(8,128)(2,1)}), bf16[384,128]{1,0:T(8,128)(2,1)}) %reduce-scatter.4.cloned.1.call-update) | async-done | bytes 98320
  329.0 1.0 copy.63
  330.1 0.7 add_convert_fusion
  330.7 3.3 all-to-all-start.1
  334.8 0.6 dynamic_slice.3
  335.4 3.0 all-to-all-done.1
  338.4 1.2 add_convert_fusion.3
  (28 shorter events, 0.3 us)
Async XLA Ops:
  7.2 283.9 %copy-start = (bf16[384,3072]{1,0:T(8,128)(2,1)S(1)}, bf16[384,3072]{1,0:T(8,128)(2,1)}, u32[]{:S(2)}) copy-start(bf16[384,3072]{1,0:T(8,128)(2,1)} %param.24) | copy-start | bytes 7077892
  10.5 18.5 %copy-start.9 = (f32[2,128]{1,0:T(2,128)S(1)}, f32[2,128]{1,0:T(2,128)}, u32[]{:S(2)}) copy-start(f32[2,128]{1,0:T(2,128)} %param.22) | copy-start | bytes 3076
  10.5 18.7 %copy-start.2 = (bf16[1,2,64,384]{3,2,1,0:T(8,128)(2,1)S(1)}, bf16[1,2,64,384]{3,2,1,0:T(8,128)(2,1)}, u32[]{:S(2)}) copy-start(bf16[1,2,64,384]{3,2,1,0:T(8,128)(2,1)} %param.17) | copy-start | bytes 294916
  10.5 19.3 %copy-start.3 = (bf16[1,2,64,384]{3,2,1,0:T(8,128)(2,1)S(1)}, bf16[1,2,64,384]{3,2,1,0:T(8,128)(2,1)}, u32[]{:S(2)}) copy-start(bf16[1,2,64,384]{3,2,1,0:T(8,128)(2,1)} %param.16) | copy-start | bytes 294916
  10.5 21.5 %copy-start.10 = (f32[128]{0:T(128)S(1)}, f32[128]{0:T(128)}, u32[]{:S(2)}) copy-start(f32[128]{0:T(128)} %param.21) | copy-start | bytes 1540
  10.5 21.6 %copy-start.5 = (bf16[1,2,16,384]{3,2,1,0:T(8,128)(2,1)S(1)}, bf16[1,2,16,384]{3,2,1,0:T(8,128)(2,1)}, u32[]{:S(2)}) copy-start(bf16[1,2,16,384]{3,2,1,0:T(8,128)(2,1)} %param.19) | copy-start | bytes 73732
  10.5 260.3 %all-to-all-start = ((bf16[32,2,80,384]{3,2,1,0:T(8,128)(2,1)}), bf16[32,2,80,384]{3,2,1,0:T(8,128)(2,1)}, u32[]{:S(2)}, u32[]{:S(2)}) async-start(bf16[32,2,80,384]{3,2,1,0:T(8,128)(2,1)} %stack.8), calls=%async_computation | async-start | bytes 7864320 | tf_op jit(solution)/shard_map/all_to_all | solution.py:70
  28.9 225.3 %all-gather.2.cloned.1.call-start = ((), (), s32[]{:S(2)}) async-start(), calls=%async_computation.3 | async-start | bytes 4055040 | tf_op jit(solution)/shard_map/all_gather | solution.py:68
  29.9 6.6 %copy-start.11 = (s32[2]{0:T(128)S(1)}, s32[2]{0:T(128)}, u32[]{:S(2)}) copy-start(s32[2]{0:T(128)} %param.27) | copy-start | bytes 28
  35.9 293.1 %reduce-scatter.4.cloned.1.call-start = ((), (), s32[]{:S(2)}) async-start(), calls=%async_computation.4 | async-start | bytes 884736
  267.9 2.0 copy-start.1
  290.9 39.1 %copy-start.8 = (f32[384]{0:T(512)S(1)}, f32[384]{0:T(512)}, u32[]{:S(2)}) copy-start(f32[384]{0:T(512)} %param.25) | copy-start | bytes 4612
  290.9 39.1 %copy-start.4 = (bf16[1,2,64,384]{3,2,1,0:T(8,128)(2,1)S(1)}, bf16[1,2,64,384]{3,2,1,0:T(8,128)(2,1)}, u32[]{:S(2)}) copy-start(bf16[1,2,64,384]{3,2,1,0:T(8,128)(2,1)} %param.15) | copy-start | bytes 294916
  290.9 39.1 %copy-start.7 = (f32[1,2,384]{2,1,0:T(2,128)S(1)}, f32[1,2,384]{2,1,0:T(2,128)}, u32[]{:S(2)}) copy-start(f32[1,2,384]{2,1,0:T(2,128)} %param.23) | copy-start | bytes 9220
  291.0 43.8 %copy-start.12 = (f32[2]{0:T(128)S(1)}, f32[2]{0:T(128)}, u32[]{:S(2)}) copy-start(f32[2]{0:T(128)} %param.26) | copy-start | bytes 28
  291.0 47.4 %copy-start.6 = (bf16[1,64,384]{2,1,0:T(8,128)(2,1)S(1)}, bf16[1,64,384]{2,1,0:T(8,128)(2,1)}, u32[]{:S(2)}) copy-start(bf16[1,64,384]{2,1,0:T(8,128)(2,1)} %param.29) | copy-start | bytes 147460
  330.7 7.6 %all-to-all-start.1 = ((bf16[1,2,64,384]{3,2,0,1:T(8,128)(2,1)}), bf16[1,2,64,384]{3,2,0,1:T(8,128)(2,1)S(1)}, u32[]{:S(2)}, u32[]{:S(2)}) async-start(bf16[1,2,64,384]{3,2,0,1:T(8,128)(2,1)} %add_convert_fusion), calls=%async_computation.1 | async-start | bytes 196608 | tf_op jit(solution)/shard_map/all_to_all | solution.py:107
Sparse Core Ops, SparseCore 0:
  36.0 218.0 all-gather.1
  293.0 35.9 reduce-scatter.3
